TPU v7x, 256 devices: a whole 4x4x8 slice. The times are simulated.
256 devices in a mesh: band: 16 (over y, x), lev: 16 (over z, core).
Axes of the slice: x: 4, y: 4, z: 8, core: 2. Of those that a mesh axis runs over, the one named last changes fastest.
Arguments:
- adj_spec: bfloat16 [64, 1280, 2, 1280], P('lev', 'band'), may hold values from -6 to 6
- wave_of_slot: int32 [1280], replicated, may hold values from 0 to 1279, each once
- legendre: bfloat16 [1280, 32, 1280], P('band'), may hold values from -0.15625 to 0.15625
- lat_weight: float32 [32], replicated, may hold values from 0.5 to 1.5
- traj: bfloat16 [64, 64, 5136], P('lev', 'band'), may hold values from -3 to 3
- traj_exp: int32 [64, 64, 4], P('lev', 'band'), may hold values from -2 to 2
- traj_order: int32 [16, 4], P('lev'), may hold values from 0 to 3, each once within a row
- lev_coef: float32 [64], P('lev'), may hold values from 0.02 to 0.2
Outputs:
- adj_out: bfloat16 [64, 1280, 2, 1280], P('lev', 'band')
Inputs may be any that keep to these rules, and one draw needn't show every extreme that they name: `wave_of_slot`: every wavenumber 0 to 1279 is held by exactly one slot. `traj_order`: each row is a permutation of 0 to 3.
All inputs are finite; a program needn't handle non-finite values.
Results may differ from a plain program's by a relative error of at most 0.0085.
Values may be sent and summed in bfloat16 or wider, within the bound.
No kernel may reach another device: no remote copies, remote signals or barrier semaphores. Data moves between devices by JAX's collectives and lax.ppermute only.
A program may use at most 128 MiB of HBM per device.

v0:
```python
import math
import jax
import jax.numpy as jnp
from jax import lax
from jax.sharding import Mesh
from jax.sharding import PartitionSpec as P

NBLK = 4
BAND = ("band_0", "band_1")


def prefix(value, axis, combine, identity):
    size, index = (lax.axis_size(axis), lax.axis_index(axis))
    everything = lax.all_gather(value.astype(jnp.bfloat16), axis)
    start = jnp.broadcast_to(jnp.asarray(identity, value.dtype), value.shape)

    def turn(k, before):
        reached = k < index
        new = combine(before, everything[k].astype(value.dtype))
        return jnp.where(reached, new, before)

    return lax.fori_loop(0, size, turn, start)


def cut_along(value, dim, size):
    lengths = value.shape
    tiles = value.reshape(*lengths[:dim], size, lengths[dim] // size, *lengths[dim + 1 :])
    return jnp.moveaxis(tiles, dim, 0)


def laid_out(tiles, dim):
    tiles = jnp.moveaxis(tiles, 0, dim)
    lengths = tiles.shape
    return tiles.reshape(*lengths[:dim], lengths[dim] * lengths[dim + 1], *lengths[dim + 2 :])


def turned_blocks(tiles, axes, turns):
    inside = tiles.shape[1:]
    whole = tiles.reshape(*(lax.axis_size(a) for a in axes), *inside)
    for k in turns:
        whole = lax.all_to_all(whole, axes[k], k, k, tiled=True)
    return whole.reshape(-1, *inside)


def one_axis_at_a_time(value, axes, turns, split_dim, concat_dim):
    tiles = cut_along(value, split_dim, lax.axis_size(axes))
    return laid_out(turned_blocks(tiles, axes, turns), concat_dim)


def trig_whole(wave_ids, lon_count):
    lon_ids = jnp.arange(lon_count, dtype=jnp.int32)
    phase_int = wave_ids[:, None] * lon_ids[None, :] % lon_count
    angle_rad = phase_int.astype(jnp.float32) * (2.0 * math.pi / lon_count)
    return jnp.stack([jnp.cos(angle_rad), -jnp.sin(angle_rad)], axis=1).astype(jnp.bfloat16)


def add_carry(earlier, later):
    return earlier + later


def body(adj_spec, wave_of_slot, legendre, lat_weight, traj, traj_exp, traj_order, lev_coef):
    highest = lax.Precision.HIGHEST
    levels = adj_spec.shape[0]
    slots = adj_spec.shape[1]
    degrees = adj_spec.shape[3]
    lat_rows = traj.shape[1]
    lon_count = traj.shape[2]
    block_width = lon_count // NBLK
    norm_scale = 1.0 / math.sqrt(degrees)
    first_slot = lax.axis_index(BAND) * slots
    waves_here = lax.dynamic_slice_in_dim(wave_of_slot, first_slot, slots)
    degree_ids = jnp.arange(degrees, dtype=jnp.int32)
    valid_mask = degree_ids[None, :] < (degrees - waves_here)[:, None]
    masked = jnp.where(valid_mask[None, :, None, :], adj_spec, jnp.zeros_like(adj_spec))
    weight_q = jnp.repeat(lat_weight, 2)
    parity_sign = jnp.where(degree_ids % 2 == 0, 1.0, -1.0).astype(jnp.bfloat16)
    stacked = jnp.stack([masked, masked * parity_sign], axis=3)
    side_values = jnp.einsum(
        "lscej,shj->lsche", stacked, legendre, preferred_element_type=jnp.float32
    )
    fourier = (side_values.reshape(levels, slots, 2, -1) * weight_q).astype(jnp.bfloat16)
    fourier_here = lax.all_to_all(fourier, BAND, split_axis=3, concat_axis=1, tiled=True)
    trig_all = trig_whole(wave_of_slot, lon_count)
    order_ids = jnp.arange(levels, dtype=jnp.int32)
    select = (traj_order[0][None, :] == order_ids[:, None]).astype(jnp.float32)
    level_coef = lev_coef[:, None, None]
    grid_list = []
    for block_id in range(NBLK):
        trig_table = trig_all[:, :, block_id * block_width : (block_id + 1) * block_width]
        grid_list.append(
            jnp.einsum(
                "lsca,scw->law", fourier_here, trig_table, preferred_element_type=jnp.float32
            )
            * norm_scale
        )
    grid_all = jnp.stack(grid_list, axis=1)
    running = jnp.cumsum(grid_all, axis=0)
    prior_sum = jnp.concatenate([jnp.zeros_like(grid_all[:1]), running[:-1]], axis=0)
    block_total = running[-1]
    group_carry = prefix(block_total, "lev", add_carry, jnp.zeros_like(block_total))
    above_all = prior_sum + group_carry[None]
    analysis = jnp.zeros((levels, degrees, 2, lat_rows), jnp.float32)
    for block_id in range(NBLK):
        lon_start = block_id * block_width
        trig_table = trig_all[:, :, lon_start : lon_start + block_width]
        exponent = jnp.exp2(traj_exp[:, :, block_id].astype(jnp.float32))
        traj_piece = (
            traj[:, :, lon_start : lon_start + block_width].astype(jnp.float32)
            * exponent[:, :, None]
        )
        traj_value = jnp.einsum("ir,raw->iaw", select, traj_piece, precision=highest)
        forcing = (
            (1.0 + jnp.tanh(traj_value))
            * (grid_all[:, block_id] + level_coef * above_all[:, block_id])
        ).astype(jnp.bfloat16)
        analysis = (
            analysis
            + jnp.einsum("law,scw->lsca", forcing, trig_table, preferred_element_type=jnp.float32)
            * norm_scale
        )
    returned = one_axis_at_a_time(analysis, BAND, (0, 1), 1, 3)
    halves = returned.reshape(levels, slots, 2, -1, 2)
    sym_part = (halves[..., 0] + halves[..., 1]).astype(jnp.bfloat16)
    anti_part = (halves[..., 0] - halves[..., 1]).astype(jnp.bfloat16)
    from_sym = jnp.einsum("lsch,shj->lscj", sym_part, legendre, preferred_element_type=jnp.float32)
    from_anti = jnp.einsum(
        "lsch,shj->lscj", anti_part, legendre, preferred_element_type=jnp.float32
    )
    result = jnp.where(degree_ids % 2 == 0, from_sym, from_anti)
    return jnp.where(valid_mask[None, :, None, :], result, 0.0).astype(jnp.bfloat16)


def solution(mesh):
    torus = Mesh(mesh.devices.reshape(4, 4, mesh.shape["lev"]), ("band_0", "band_1", "lev"))
    return jax.shard_map(
        body,
        mesh=torus,
        in_specs=(
            P("lev", BAND, None, None),
            P(),
            P(BAND, None, None),
            P(),
            P("lev", BAND, None),
            P("lev", BAND, None),
            P("lev", None),
            P("lev"),
        ),
        out_specs=P("lev", BAND, None, None),
        check_vma=False,
    )
```

profile of v0, /device:TPU:2, one launch (start us, length us, event | category | flops | bytes accessed | tf_op | source)
XLA Modules:
  0.0 222.6 jit_solution(7207689764464458243)
XLA Ops:
  0.0 0.8 dynamic-slice_subtract_fusion
  0.8 0.1 iota_compare_fusion
  0.9 3.5 %fusion.94 = (bf16[4,80,2,1,1280]{4,0,3,2,1:T(4,128)(2,1)S(1)}, bf16[4,80,2,1,1280]{4,0,3,2,1:T(4,128)(2,1)S(1)}) fusion(bf16[4,80,2,1280]{3,2,1,0:T(2,128)(2,1)} %param.10, pred[80,1280]{1,0:T(8,128)(4,1)S(1)} %iota_compare_fusion, bf16[1280]{0:T(1024)(128)(2,1)S(1)} %select_convert_fusion.1), kind=kLoop, calls=%fused_computation.79 | loop fusion | flops 1638400 | bytes 5020160 | tf_op jit(solution)/shard_map/stack | solution.py:77
  4.5 6.2 %fusion.89 = f32[4,80,2,32,2]{3,0,4,2,1:T(4,128)S(1)} fusion(bf16[80,32,1280]{2,1,0:T(8,128)(2,1)} %param.12, bf16[4,80,2,1,1280]{4,0,3,2,1:T(4,128)(2,1)S(1)} %get-tuple-element.129, bf16[4,80,2,1,1280]{4,0,3,2,1:T(4,128)(2,1)S(1)} %get-tuple-element.128), kind=kOutput, calls=%fused_computation.78 | convolution fusion | flops 111411200 | bytes 9994240 | tf_op jit(solution)/shard_map/lscej,shj->lsche/dot_general | solution.py:78
  10.6 0.3 copy.69
  11.0 0.1 mul.183
  11.1 0.1 multiply_convert_fusion
  11.2 0.8 copy.70
  12.0 7.5 %all-to-all-start = ((bf16[4,80,2,64]{1,2,0,3:T(2,128)(2,1)}), bf16[4,80,2,64]{1,2,0,3:T(2,128)(2,1)S(1)}, u32[]{:S(2)}, u32[]{:S(2)}) async-start(bf16[4,80,2,64]{1,2,0,3:T(2,128)(2,1)} %copy.70), calls=%async_computation | async-start | bytes 262144 | tf_op jit(solution)/shard_map/all_to_all | solution.py:82
  19.5 109.3 %cosine_convert_fusion = (bf16[1280,1,5136]{0,2,1:T(8,128)(2,1)S(1)}, bf16[1280,1,5136]{0,2,1:T(8,128)(2,1)S(1)}) fusion(s32[1280]{0:T(1024)S(1)} %copy-done.3), kind=kLoop, calls=%fused_computation.11 | loop fusion | flops 78888960 | bytes 26301440 | tf_op jit(solution)/shard_map/convert.2
  128.8 0.2 exponential_reduce_fusion.3
  129.0 10.5 %fusion.6 = (bf16[1280,2,1284]{0,2,1:T(8,128)(2,1)}, bf16[1280,2,1284]{0,2,1:T(8,128)(2,1)}, bf16[1280,2,1284]{0,2,1:T(8,128)(2,1)}, bf16[1280,2,1284]{0,2,1:T(8,128)(2,1)}) fusion(bf16[1280,1,5136]{0,2,1:T(8,128)(2,1)S(1)} %get-tuple-element.136, bf16[1280,1,5136]{0,2,1:T(8,128)(2,1)S(1)} %get-tuple-element.137), kind=kLoop, calls=%fused_computation.17 | loop fusion | flops 52592640 | bytes 52592640 | tf_op jit(solution)/shard_map/stack | solution.py:54
  139.5 0.2 convert_multiply_fusion.3
  139.8 0.2 reshape.151
  140.0 5.0 %fusion.74 = f32[4,4,1284]{2,0,1:T(4,128)S(1)} fusion(bf16[4,1280,2,4]{1,0,2,3:T(4,128)(2,1)S(1)} %reshape.151, bf16[1280,2,1284]{0,2,1:T(8,128)(2,1)} %get-tuple-element.126), kind=kOutput, calls=%fused_computation.59 | convolution fusion | flops 105205824 | bytes 6738176 | tf_op jit(solution)/shard_map/lsca,scw->law/dot_general | solution.py:91
  145.0 5.0 %fusion.68 = f32[4,4,1284]{2,0,1:T(4,128)S(1)} fusion(bf16[4,1280,2,4]{1,0,2,3:T(4,128)(2,1)S(1)} %reshape.151, bf16[1280,2,1284]{0,2,1:T(8,128)(2,1)} %get-tuple-element.127), kind=kOutput, calls=%fused_computation.57 | convolution fusion | flops 105205824 | bytes 6738176 | tf_op jit(solution)/shard_map/lsca,scw->law/dot_general | solution.py:91
  150.0 2.0 fusion.62
  152.0 2.0 fusion.56
  154.0 0.1 pad_maximum_fusion.1
  154.1 0.5 reduce_window_sum.11
  154.6 0.1 slice.160
  154.7 22.2 %all_gather.4 = bf16[16,4,4,1284]{3,2,1,0:T(4,128)(2,1)S(1)} all-gather(bf16[1,4,4,1284]{3,2,1,0:T(4,128)(2,1)S(1)} %copy.77), channel_id=1, replica_groups=mesh['band_0'=4,'band_1'=4,'lev'=16] {'lev'}, dimensions={0}, use_global_device_ids=true | all-gather | bytes 698496 | tf_op jit(solution)/shard_map/all_gather | solution.py:14
  176.9 1.7 while.14
  176.9 0.1 add_select_fusion.4
  177.0 0.1 add_select_fusion.4
  177.1 0.1 add_select_fusion.4
  177.2 0.1 add_select_fusion.4
  177.3 0.1 add_select_fusion.4
  177.4 0.1 add_select_fusion.4
  177.5 0.1 add_select_fusion.4
  177.6 0.1 add_select_fusion.4
  177.7 0.1 add_select_fusion.4
  177.8 0.1 add_select_fusion.4
  177.9 0.1 add_select_fusion.4
  178.0 0.1 add_select_fusion.4
  178.2 0.1 add_select_fusion.4
  178.3 0.1 add_select_fusion.4
  178.4 0.1 add_select_fusion.4
  178.5 0.1 add_select_fusion.4
  178.6 0.2 pad_add_fusion
  178.8 0.2 fusion.88
  179.0 4.3 %fusion.8 = f32[1280,2,4,4]{0,3,2,1:T(4,128)S(1)} fusion(bf16[1280,2,1284]{0,2,1:T(8,128)(2,1)} %get-tuple-element.126, bf16[4,4,1284]{2,0,1:T(4,128)(2,1)S(1)} %fusion.88), kind=kOutput, calls=%fused_computation.20 | convolution fusion | flops 105185280 | bytes 6779008 | tf_op jit(solution)/shard_map/law,scw->lsca/dot_general | solution.py:118
  183.3 0.2 fusion.87
  183.6 1.2 fusion.10
  184.8 0.2 fusion.86
  185.1 0.4 slice-done.5
  185.5 1.2 fusion.12
  186.7 0.2 fusion.85
  187.0 0.4 slice-done.3
  187.4 1.2 fusion.50
  188.7 0.2 reshape.131
  188.9 0.1 copy.86
  189.0 11.2 %all_to_all.28 = f32[4,4,4,80,2,4]{3,5,1,4,2,0:T(4,128)S(1)} all-to-all(f32[4,4,4,80,2,4]{3,5,1,4,2,0:T(4,128)S(1)} %copy.86), channel_id=1, replica_groups=mesh['band_0'=4,'band_1'=4,'lev'=16] {'band_0'}, dimensions={0} | all-to-all | bytes 327680 | tf_op jit(solution)/shard_map/all_to_all | solution.py:41
  200.3 0.8 copy.87
  201.0 4.8 %all-to-all-start.2 = ((f32[4,4,4,80,2,4]{3,5,0,4,2,1:T(4,128)}), f32[4,4,4,80,2,4]{3,5,0,4,2,1:T(4,128)S(1)}, u32[]{:S(2)}, u32[]{:S(2)}) async-start(f32[4,4,4,80,2,4]{3,5,0,4,2,1:T(4,128)} %copy.87), calls=%async_computation.2 | async-start | bytes 524288 | tf_op jit(solution)/shard_map/all_to_all | solution.py:41
  205.8 5.2 %all-to-all-done.2 = f32[4,4,4,80,2,4]{3,5,0,4,2,1:T(4,128)S(1)} async-done(((f32[4,4,4,80,2,4]{3,5,0,4,2,1:T(4,128)}), f32[4,4,4,80,2,4]{3,5,0,4,2,1:T(4,128)S(1)}, u32[]{:S(2)}, u32[]{:S(2)}) %all-to-all-start.2) | async-done | bytes 163872 | tf_op jit(solution)/shard_map/all_to_all | solution.py:41
  211.0 0.2 copy.88
  211.2 0.1 copy.89
  211.3 0.3 add_convert_fusion
  211.6 0.2 copy.111
  211.8 3.8 %fusion.26 = bf16[80,4,2,1280]{3,1,2,0:T(4,128)(2,1)S(1)} fusion(bf16[80,32,1280]{2,1,0:T(8,128)(2,1)} %param.12, bf16[4,80,2,32,1]{3,0,2,1,4:T(4,128)(2,1)S(1)} %copy.111), kind=kOutput, calls=%fused_computation.38 | convolution fusion | flops 52428800 | bytes 8232960 | tf_op jit(solution)/shard_map/lsch,shj->lscj/dot_general | solution.py:126
  215.6 0.2 copy.110
  215.8 4.4 %fusion.35 = bf16[4,80,2,1280]{3,0,2,1:T(4,128)(2,1)S(1)} fusion(bf16[80,4,2,1280]{3,1,2,0:T(4,128)(2,1)S(1)} %fusion.26, bf16[80,32,1280]{2,1,0:T(8,128)(2,1)} %param.12, pred[1280]{0:T(1024)(128)(4,1)S(1)} %fusion.117, pred[80,1280]{1,0:T(8,128)(4,1)S(1)} %iota_compare_fusion, bf16[4,80,2,32,1]{3,0,2,1,4:T(4,128)(2,1)S(1)} %copy.110), kind=kOutput, calls=%fused_computation.46 | convolution fusion | flops 54067200 | bytes 9975040 | tf_op jit(solution)/shard_map/lsch,shj->lscj/dot_general | solution.py:125
  220.2 2.4 %copy.92 = bf16[4,80,2,1280]{3,2,1,0:T(2,128)(2,1)} copy(bf16[4,80,2,1280]{3,0,2,1:T(4,128)(2,1)S(1)} %fusion.35) | data formatting | bytes 3276800 | tf_op jit(solution)/shard_map/convert_element_type | solution.py:130
  (41 shorter events, 0.2 us)
Async XLA Ops:
  4.5 6.5 %copy-start.4 = (f32[32]{0:T(128)S(1)}, f32[32]{0:T(128)}, u32[]{:S(2)}) copy-start(f32[32]{0:T(128)} %param.13) | copy-start | bytes 388
  4.5 15.0 %copy-start.3 = (s32[1280]{0:T(1024)S(1)}, s32[1280]{0:T(1024)}, u32[]{:S(2)}) copy-start(s32[1280]{0:T(1024)} %param.11) | copy-start | bytes 15364
  12.0 127.7 %all-to-all-start = ((bf16[4,80,2,64]{1,2,0,3:T(2,128)(2,1)}), bf16[4,80,2,64]{1,2,0,3:T(2,128)(2,1)S(1)}, u32[]{:S(2)}, u32[]{:S(2)}) async-start(bf16[4,80,2,64]{1,2,0,3:T(2,128)(2,1)} %copy.70), calls=%async_computation | async-start | bytes 262144 | tf_op jit(solution)/shard_map/all_to_all | solution.py:82
  19.5 109.3 %copy-start.2 = (s32[4,4,4]{2,1,0:T(4,128)S(1)}, s32[4,4,4]{2,1,0:T(4,128)}, u32[]{:S(2)}) copy-start(s32[4,4,4]{2,1,0:T(4,128)} %param.15) | copy-start | bytes 772
  129.0 10.5 %copy-start.1 = (bf16[4,4,5136]{2,1,0:T(4,128)(2,1)S(1)}, bf16[4,4,5136]{2,1,0:T(4,128)(2,1)}, u32[]{:S(2)}) copy-start(bf16[4,4,5136]{2,1,0:T(4,128)(2,1)} %param.14) | copy-start | bytes 493060
  140.0 10.0 %copy-start = (bf16[1280,2,1284]{0,2,1:T(8,128)(2,1)S(1)}, bf16[1280,2,1284]{0,2,1:T(8,128)(2,1)}, u32[]{:S(2)}) copy-start(bf16[1280,2,1284]{0,2,1:T(8,128)(2,1)} %get-tuple-element.125) | copy-start | bytes 19722244
  140.0 12.0 %slice-start = ((s8[6594560]{0:T(1024)(128)(4,1)}), s8[4194304]{0:T(1024)(128)(4,1)S(1)}, s32[]{:S(2)}) async-start(s8[6594560]{0:T(1024)(128)(4,1)} %bitcast.188), calls=%async_computation.3 | async-start | bytes 8388608
  145.0 7.0 %slice-start.1 = ((s8[6594560]{0:T(1024)(128)(4,1)}), s8[2400256]{0:T(1024)(128)(4,1)S(1)}, s32[]{:S(2)}) async-start(s8[6594560]{0:T(1024)(128)(4,1)} %bitcast.188), calls=%async_computation.4 | async-start | bytes 4800512
  151.9 26.8 %copy-start.5 = (f32[4]{0:T(128)S(1)}, f32[4]{0:T(128)}, u32[]{:S(2)}) copy-start(f32[4]{0:T(128)} %param.17) | copy-start | bytes 52
  151.9 26.8 %copy-start.6 = (s32[1,4]{1,0:T(1,128)S(1)}, s32[1,4]{1,0:T(1,128)}, u32[]{:S(2)}) copy-start(s32[1,4]{1,0:T(1,128)} %param.16) | copy-start | bytes 52
  178.6 5.0 %slice-start.6 = ((s8[6594560]{0:T(1024)(128)(4,1)}), s8[4194304]{0:T(1024)(128)(4,1)S(1)}, s32[]{:S(2)}) async-start(s8[6594560]{0:T(1024)(128)(4,1)} %bitcast.194), calls=%async_computation.9 | async-start | bytes 8388608
  179.0 4.6 %slice-start.7 = ((s8[6594560]{0:T(1024)(128)(4,1)}), s8[2400256]{0:T(1024)(128)(4,1)S(1)}, s32[]{:S(2)}) async-start(s8[6594560]{0:T(1024)(128)(4,1)} %bitcast.194), calls=%async_computation.10 | async-start | bytes 4800512
  179.0 6.1 %slice-start.4 = ((s8[6594560]{0:T(1024)(128)(4,1)}), s8[4194304]{0:T(1024)(128)(4,1)S(1)}, s32[]{:S(2)}) async-start(s8[6594560]{0:T(1024)(128)(4,1)} %bitcast.192), calls=%async_computation.7 | async-start | bytes 8388608
  183.6 1.9 slice-start.5
  183.6 3.4 %slice-start.2 = ((s8[6594560]{0:T(1024)(128)(4,1)}), s8[4194304]{0:T(1024)(128)(4,1)S(1)}, s32[]{:S(2)}) async-start(s8[6594560]{0:T(1024)(128)(4,1)} %bitcast.190), calls=%async_computation.5 | async-start | bytes 8388608
  185.5 1.9 slice-start.3
  201.0 10.0 %all-to-all-start.2 = ((f32[4,4,4,80,2,4]{3,5,0,4,2,1:T(4,128)}), f32[4,4,4,80,2,4]{3,5,0,4,2,1:T(4,128)S(1)}, u32[]{:S(2)}, u32[]{:S(2)}) async-start(f32[4,4,4,80,2,4]{3,5,0,4,2,1:T(4,128)} %copy.87), calls=%async_computation.2 | async-start | bytes 524288 | tf_op jit(solution)/shard_map/all_to_all | solution.py:41
where the time goes:
time: 223 us
  other arithmetic  127 us (57%)
  matrix products  37.2 us (17%)
  blocking collectives  33.4 us (15%)
  starting transfers between devices  12.3 us (6%)
  local copies, waits for them, and re-layouts  6.71 us (3%)
  waiting for transfers between devices  5.22 us (2%)
    another operation x1, other arithmetic  109 us
    all_gather x1, blocking collectives, prefix(): everything = lax.all_gather(value.astype(jnp.bfloat16), axis)  22.2 us
    dot_general x4, matrix products, body(): jnp.einsum('lsca,scw->law', fourier_here, trig_table, preferred_element_t...  13.9 us
    all_to_all x1, blocking collectives, turned_blocks(): whole = lax.all_to_all(whole, axes[k], k, k, tiled=True)  11.2 us
    another operation x1, other arithmetic, trig_whole(): jnp.stack([jnp.cos(angle_rad), -jnp.sin(angle_rad)], axis=1)  10.5 us
    dot_general x4, matrix products, body(): jnp.einsum('law,scw->lsca', forcing, trig_table, preferred_element_type=j...  8 us
    all_to_all x1, starting transfers between devices, body(): lax.all_to_all(fourier, BAND, split_axis=3, concat_axis=1, tiled=True)  7.48 us
    dot_general x1, matrix products, body(): jnp.einsum('lscej,shj->lsche', stacked, legendre, preferred_element_type=...  6.16 us
  transfers between devices with their start and end apart: 2, of which 1 were waited for; matrix products, arithmetic and copies ran while one was open for 54% of the time, Pallas kernels for 0%

commit v1 on v0

--- a/solution.py
+++ b/solution.py
@@ -79,7 +79,15 @@
         "lscej,shj->lsche", stacked, legendre, preferred_element_type=jnp.float32
     )
     fourier = (side_values.reshape(levels, slots, 2, -1) * weight_q).astype(jnp.bfloat16)
-    fourier_here = lax.all_to_all(fourier, BAND, split_axis=3, concat_axis=1, tiled=True)
+    fourier_here = jnp.concatenate(
+        lax.all_to_all(
+            jnp.stack(jnp.split(fourier, lax.axis_size(BAND), axis=3)),
+            BAND,
+            split_axis=0,
+            concat_axis=0,
+        ),
+        axis=1,
+    )
     trig_all = trig_whole(wave_of_slot, lon_count)
     order_ids = jnp.arange(levels, dtype=jnp.int32)
     select = (traj_order[0][None, :] == order_ids[:, None]).astype(jnp.float32)

time: 223 us -> 232 us (1.040)
  local copies, waits for them, and re-layouts: 6.71 us -> 15.6 us
    unnamed x30 -> x45, local copies, waits for them, and re-layouts: 0.96 us -> 10 us
  transfers between devices with their start and end apart: 2 -> 2, of which waited for: 1 -> 1; matrix products, arithmetic and copies ran while one was open for 54% -> 52% of each run, Pallas kernels for 0% -> 0%
where the time goes in v1:
time: 232 us
  other arithmetic  127 us (55%)
  matrix products  37.2 us (16%)
  blocking collectives  33.4 us (14%)
  local copies, waits for them, and re-layouts  15.6 us (7%)
  starting transfers between devices  12.3 us (5%)
  waiting for transfers between devices  5.22 us (2%)
    another operation x1, other arithmetic  109 us
    all_gather x1, blocking collectives, prefix(): everything = lax.all_gather(value.astype(jnp.bfloat16), axis)  22.2 us
    dot_general x4, matrix products, body(): jnp.einsum('lsca,scw->law', fourier_here, trig_table, preferred_element_t...  13.9 us
    all_to_all x1, blocking collectives, turned_blocks(): whole = lax.all_to_all(whole, axes[k], k, k, tiled=True)  11.2 us
    another operation x1, other arithmetic, trig_whole(): jnp.stack([jnp.cos(angle_rad), -jnp.sin(angle_rad)], axis=1)  10.5 us
    unnamed x45, local copies, waits for them, and re-layouts  10 us
    dot_general x4, matrix products, body(): jnp.einsum('law,scw->lsca', forcing, trig_table, preferred_element_type=j...  8 us
    all_to_all x1, starting transfers between devices, body(): lax.all_to_all(jnp.stack(jnp.split(fourier, lax.axis_size(BAND), axis=3))...  7.48 us
  transfers between devices with their start and end apart: 2, of which 1 were waited for; matrix products, arithmetic and copies ran while one was open for 52% of the time, Pallas kernels for 0%

profile of v1, /device:TPU:2, one launch (start us, length us, event | category | flops | bytes accessed | tf_op | source)
XLA Modules:
  0.0 231.5 jit_solution(15794193014706480578)
XLA Ops:
  0.0 0.8 dynamic-slice_subtract_fusion
  0.8 0.1 iota_compare_fusion
  0.9 3.5 %fusion.94 = (bf16[4,80,2,1,1280]{4,0,3,2,1:T(4,128)(2,1)S(1)}, bf16[4,80,2,1,1280]{4,0,3,2,1:T(4,128)(2,1)S(1)}) fusion(bf16[4,80,2,1280]{3,2,1,0:T(2,128)(2,1)} %param.10, pred[80,1280]{1,0:T(8,128)(4,1)S(1)} %iota_compare_fusion, bf16[1280]{0:T(1024)(128)(2,1)S(1)} %select_convert_fusion.1), kind=kLoop, calls=%fused_computation.79 | loop fusion | flops 1638400 | bytes 5020160 | tf_op jit(solution)/shard_map/stack | solution.py:77
  4.5 6.2 %fusion.89 = f32[4,80,2,32,2]{3,0,4,2,1:T(4,128)S(1)} fusion(bf16[80,32,1280]{2,1,0:T(8,128)(2,1)} %param.12, bf16[4,80,2,1,1280]{4,0,3,2,1:T(4,128)(2,1)S(1)} %get-tuple-element.129, bf16[4,80,2,1,1280]{4,0,3,2,1:T(4,128)(2,1)S(1)} %get-tuple-element.128), kind=kOutput, calls=%fused_computation.78 | convolution fusion | flops 111411200 | bytes 9994240 | tf_op jit(solution)/shard_map/lscej,shj->lsche/dot_general | solution.py:78
  10.6 0.3 copy.82
  11.0 0.1 mul.183
  11.1 0.1 multiply_convert_fusion
  11.2 0.6 constant_dynamic-update-slice_fusion.15
  11.8 0.6 constant_dynamic-update-slice_fusion.14
  12.4 0.6 constant_dynamic-update-slice_fusion.13
  13.1 0.6 constant_dynamic-update-slice_fusion.12
  13.7 0.6 constant_dynamic-update-slice_fusion.11
  14.3 0.6 constant_dynamic-update-slice_fusion.10
  14.9 0.6 constant_dynamic-update-slice_fusion.9
  15.5 0.6 constant_dynamic-update-slice_fusion.8
  16.1 0.6 constant_dynamic-update-slice_fusion.7
  16.7 0.6 constant_dynamic-update-slice_fusion.6
  17.3 0.6 constant_dynamic-update-slice_fusion.5
  17.9 0.6 constant_dynamic-update-slice_fusion.4
  18.5 0.6 constant_dynamic-update-slice_fusion.3
  19.1 0.6 constant_dynamic-update-slice_fusion.2
  19.7 0.6 constant_dynamic-update-slice_fusion.1
  20.3 0.6 constant_dynamic-update-slice_fusion
  20.9 7.5 %all-to-all-start = ((bf16[16,4,80,2,4]{2,4,3,1,0:T(4,128)(2,1)}), bf16[16,4,80,2,4]{2,4,3,1,0:T(4,128)(2,1)S(1)}, u32[]{:S(2)}, u32[]{:S(2)}) async-start(bf16[16,4,80,2,4]{2,4,3,1,0:T(4,128)(2,1)} %constant_dynamic-update-slice_fusion), calls=%async_computation | async-start | bytes 262144 | tf_op jit(solution)/shard_map/all_to_all | solution.py:83
  28.4 109.3 %cosine_convert_fusion = (bf16[1280,1,5136]{0,2,1:T(8,128)(2,1)S(1)}, bf16[1280,1,5136]{0,2,1:T(8,128)(2,1)S(1)}) fusion(s32[1280]{0:T(1024)S(1)} %copy-done.3), kind=kLoop, calls=%fused_computation.11 | loop fusion | flops 78888960 | bytes 26301440 | tf_op jit(solution)/shard_map/convert.2
  137.7 0.2 exponential_reduce_fusion.3
  137.9 10.5 %fusion.6 = (bf16[1280,2,1284]{0,2,1:T(8,128)(2,1)}, bf16[1280,2,1284]{0,2,1:T(8,128)(2,1)}, bf16[1280,2,1284]{0,2,1:T(8,128)(2,1)}, bf16[1280,2,1284]{0,2,1:T(8,128)(2,1)}) fusion(bf16[1280,1,5136]{0,2,1:T(8,128)(2,1)S(1)} %get-tuple-element.136, bf16[1280,1,5136]{0,2,1:T(8,128)(2,1)S(1)} %get-tuple-element.137), kind=kLoop, calls=%fused_computation.17 | loop fusion | flops 52592640 | bytes 52592640 | tf_op jit(solution)/shard_map/stack | solution.py:54
  148.4 0.2 convert_multiply_fusion.3
  148.7 0.2 reshape.159
  148.9 5.0 %fusion.74 = f32[4,4,1284]{2,0,1:T(4,128)S(1)} fusion(bf16[4,1280,2,4]{1,0,2,3:T(4,128)(2,1)S(1)} %reshape.159, bf16[1280,2,1284]{0,2,1:T(8,128)(2,1)} %get-tuple-element.126), kind=kOutput, calls=%fused_computation.59 | convolution fusion | flops 105205824 | bytes 6738176 | tf_op jit(solution)/shard_map/lsca,scw->law/dot_general | solution.py:99
  153.9 5.0 %fusion.68 = f32[4,4,1284]{2,0,1:T(4,128)S(1)} fusion(bf16[4,1280,2,4]{1,0,2,3:T(4,128)(2,1)S(1)} %reshape.159, bf16[1280,2,1284]{0,2,1:T(8,128)(2,1)} %get-tuple-element.127), kind=kOutput, calls=%fused_computation.57 | convolution fusion | flops 105205824 | bytes 6738176 | tf_op jit(solution)/shard_map/lsca,scw->law/dot_general | solution.py:99
  158.9 2.0 fusion.62
  160.9 2.0 fusion.56
  163.0 0.5 reduce_window_sum.11
  163.5 0.1 slice.160
  163.6 22.2 %all_gather.4 = bf16[16,4,4,1284]{3,2,1,0:T(4,128)(2,1)S(1)} all-gather(bf16[1,4,4,1284]{3,2,1,0:T(4,128)(2,1)S(1)} %copy.88), channel_id=1, replica_groups=mesh['band_0'=4,'band_1'=4,'lev'=16] {'lev'}, dimensions={0}, use_global_device_ids=true | all-gather | bytes 698496 | tf_op jit(solution)/shard_map/all_gather | solution.py:14
  185.8 1.7 while.14
  185.9 0.1 add_select_fusion.4
  186.3 0.1 add_select_fusion.4
  187.5 0.2 pad_add_fusion
  187.7 0.2 fusion.88
  187.9 4.3 %fusion.8 = f32[1280,2,4,4]{0,3,2,1:T(4,128)S(1)} fusion(bf16[1280,2,1284]{0,2,1:T(8,128)(2,1)} %get-tuple-element.126, bf16[4,4,1284]{2,0,1:T(4,128)(2,1)S(1)} %fusion.88), kind=kOutput, calls=%fused_computation.20 | convolution fusion | flops 105185280 | bytes 6779008 | tf_op jit(solution)/shard_map/law,scw->lsca/dot_general | solution.py:126
  192.2 0.2 fusion.87
  192.5 1.2 fusion.10
  193.7 0.2 fusion.86
  194.0 0.4 slice-done.5
  194.4 1.2 fusion.12
  195.7 0.2 fusion.85
  195.9 0.4 slice-done.3
  196.4 1.2 fusion.50
  197.6 0.2 reshape.139
  197.8 0.1 copy.97
  197.9 11.2 %all_to_all.15 = f32[4,4,4,80,2,4]{3,5,1,4,2,0:T(4,128)S(1)} all-to-all(f32[4,4,4,80,2,4]{3,5,1,4,2,0:T(4,128)S(1)} %copy.97), channel_id=1, replica_groups=mesh['band_0'=4,'band_1'=4,'lev'=16] {'band_0'}, dimensions={0} | all-to-all | bytes 327680 | tf_op jit(solution)/shard_map/all_to_all | solution.py:41
  209.2 0.8 copy.98
  209.9 4.8 %all-to-all-start.2 = ((f32[4,4,4,80,2,4]{3,5,0,4,2,1:T(4,128)}), f32[4,4,4,80,2,4]{3,5,0,4,2,1:T(4,128)S(1)}, u32[]{:S(2)}, u32[]{:S(2)}) async-start(f32[4,4,4,80,2,4]{3,5,0,4,2,1:T(4,128)} %copy.98), calls=%async_computation.2 | async-start | bytes 524288 | tf_op jit(solution)/shard_map/all_to_all | solution.py:41
  214.7 5.2 %all-to-all-done.2 = f32[4,4,4,80,2,4]{3,5,0,4,2,1:T(4,128)S(1)} async-done(((f32[4,4,4,80,2,4]{3,5,0,4,2,1:T(4,128)}), f32[4,4,4,80,2,4]{3,5,0,4,2,1:T(4,128)S(1)}, u32[]{:S(2)}, u32[]{:S(2)}) %all-to-all-start.2) | async-done | bytes 163872 | tf_op jit(solution)/shard_map/all_to_all | solution.py:41
  220.0 0.2 copy.99
  220.1 0.1 copy.100
  220.2 0.3 add_convert_fusion
  220.5 0.2 copy.122
  220.7 3.8 %fusion.26 = bf16[80,4,2,1280]{3,1,2,0:T(4,128)(2,1)S(1)} fusion(bf16[80,32,1280]{2,1,0:T(8,128)(2,1)} %param.12, bf16[4,80,2,32,1]{3,0,2,1,4:T(4,128)(2,1)S(1)} %copy.122), kind=kOutput, calls=%fused_computation.38 | convolution fusion | flops 52428800 | bytes 8232960 | tf_op jit(solution)/shard_map/lsch,shj->lscj/dot_general | solution.py:134
  224.5 0.2 copy.121
  224.7 4.4 %fusion.35 = bf16[4,80,2,1280]{3,0,2,1:T(4,128)(2,1)S(1)} fusion(bf16[80,4,2,1280]{3,1,2,0:T(4,128)(2,1)S(1)} %fusion.26, bf16[80,32,1280]{2,1,0:T(8,128)(2,1)} %param.12, pred[1280]{0:T(1024)(128)(4,1)S(1)} %fusion.117, pred[80,1280]{1,0:T(8,128)(4,1)S(1)} %iota_compare_fusion, bf16[4,80,2,32,1]{3,0,2,1,4:T(4,128)(2,1)S(1)} %copy.121), kind=kOutput, calls=%fused_computation.46 | convolution fusion | flops 54067200 | bytes 9975040 | tf_op jit(solution)/shard_map/lsch,shj->lscj/dot_general | solution.py:133
  229.1 2.4 %copy.103 = bf16[4,80,2,1280]{3,2,1,0:T(2,128)(2,1)} copy(bf16[4,80,2,1280]{3,0,2,1:T(4,128)(2,1)S(1)} %fusion.35) | data formatting | bytes 3276800 | tf_op jit(solution)/shard_map/convert_element_type | solution.py:138
  (55 shorter events, 1.6 us)
Async XLA Ops:
  4.5 6.5 %copy-start.4 = (f32[32]{0:T(128)S(1)}, f32[32]{0:T(128)}, u32[]{:S(2)}) copy-start(f32[32]{0:T(128)} %param.13) | copy-start | bytes 388
  4.5 24.0 %copy-start.3 = (s32[1280]{0:T(1024)S(1)}, s32[1280]{0:T(1024)}, u32[]{:S(2)}) copy-start(s32[1280]{0:T(1024)} %param.11) | copy-start | bytes 15364
  20.9 127.7 %all-to-all-start = ((bf16[16,4,80,2,4]{2,4,3,1,0:T(4,128)(2,1)}), bf16[16,4,80,2,4]{2,4,3,1,0:T(4,128)(2,1)S(1)}, u32[]{:S(2)}, u32[]{:S(2)}) async-start(bf16[16,4,80,2,4]{2,4,3,1,0:T(4,128)(2,1)} %constant_dynamic-update-slice_fusion), calls=%async_computation | async-start | bytes 262144 | tf_op jit(solution)/shard_map/all_to_all | solution.py:83
  28.4 109.3 %copy-start.2 = (s32[4,4,4]{2,1,0:T(4,128)S(1)}, s32[4,4,4]{2,1,0:T(4,128)}, u32[]{:S(2)}) copy-start(s32[4,4,4]{2,1,0:T(4,128)} %param.15) | copy-start | bytes 772
  137.9 10.5 %copy-start.1 = (bf16[4,4,5136]{2,1,0:T(4,128)(2,1)S(1)}, bf16[4,4,5136]{2,1,0:T(4,128)(2,1)}, u32[]{:S(2)}) copy-start(bf16[4,4,5136]{2,1,0:T(4,128)(2,1)} %param.14) | copy-start | bytes 493060
  148.9 10.0 %copy-start = (bf16[1280,2,1284]{0,2,1:T(8,128)(2,1)S(1)}, bf16[1280,2,1284]{0,2,1:T(8,128)(2,1)}, u32[]{:S(2)}) copy-start(bf16[1280,2,1284]{0,2,1:T(8,128)(2,1)} %get-tuple-element.125) | copy-start | bytes 19722244
  148.9 12.0 %slice-start = ((s8[6594560]{0:T(1024)(128)(4,1)}), s8[4194304]{0:T(1024)(128)(4,1)S(1)}, s32[]{:S(2)}) async-start(s8[6594560]{0:T(1024)(128)(4,1)} %bitcast.250), calls=%async_computation.3 | async-start | bytes 8388608
  153.9 7.0 %slice-start.1 = ((s8[6594560]{0:T(1024)(128)(4,1)}), s8[2400256]{0:T(1024)(128)(4,1)S(1)}, s32[]{:S(2)}) async-start(s8[6594560]{0:T(1024)(128)(4,1)} %bitcast.250), calls=%async_computation.4 | async-start | bytes 4800512
  160.8 26.8 %copy-start.5 = (f32[4]{0:T(128)S(1)}, f32[4]{0:T(128)}, u32[]{:S(2)}) copy-start(f32[4]{0:T(128)} %param.17) | copy-start | bytes 52
  160.9 26.8 %copy-start.6 = (s32[1,4]{1,0:T(1,128)S(1)}, s32[1,4]{1,0:T(1,128)}, u32[]{:S(2)}) copy-start(s32[1,4]{1,0:T(1,128)} %param.16) | copy-start | bytes 52
  187.5 5.0 %slice-start.6 = ((s8[6594560]{0:T(1024)(128)(4,1)}), s8[4194304]{0:T(1024)(128)(4,1)S(1)}, s32[]{:S(2)}) async-start(s8[6594560]{0:T(1024)(128)(4,1)} %bitcast.256), calls=%async_computation.9 | async-start | bytes 8388608
  187.9 4.6 %slice-start.7 = ((s8[6594560]{0:T(1024)(128)(4,1)}), s8[2400256]{0:T(1024)(128)(4,1)S(1)}, s32[]{:S(2)}) async-start(s8[6594560]{0:T(1024)(128)(4,1)} %bitcast.256), calls=%async_computation.10 | async-start | bytes 4800512
  187.9 6.1 %slice-start.4 = ((s8[6594560]{0:T(1024)(128)(4,1)}), s8[4194304]{0:T(1024)(128)(4,1)S(1)}, s32[]{:S(2)}) async-start(s8[6594560]{0:T(1024)(128)(4,1)} %bitcast.254), calls=%async_computation.7 | async-start | bytes 8388608
  192.5 1.9 slice-start.5
  192.5 3.4 %slice-start.2 = ((s8[6594560]{0:T(1024)(128)(4,1)}), s8[4194304]{0:T(1024)(128)(4,1)S(1)}, s32[]{:S(2)}) async-start(s8[6594560]{0:T(1024)(128)(4,1)} %bitcast.252), calls=%async_computation.5 | async-start | bytes 8388608
  194.4 1.9 slice-start.3
  209.9 10.0 %all-to-all-start.2 = ((f32[4,4,4,80,2,4]{3,5,0,4,2,1:T(4,128)}), f32[4,4,4,80,2,4]{3,5,0,4,2,1:T(4,128)S(1)}, u32[]{:S(2)}, u32[]{:S(2)}) async-start(f32[4,4,4,80,2,4]{3,5,0,4,2,1:T(4,128)} %copy.98), calls=%async_computation.2 | async-start | bytes 524288 | tf_op jit(solution)/shard_map/all_to_all | solution.py:41
